TPU v7x, 32 devices: a whole 2x2x4 slice. The times are simulated.
32 devices in a mesh: dp: 4 (over y, core), ctx: 4 (over z), tsp: 2 (over x).
Axes of the slice: x: 2, y: 2, z: 4, core: 2. Of those that a mesh axis runs over, the one named last changes fastest.
Arguments:
- grad_out: bfloat16 [4, 1024, 8192], P('dp', 'ctx', 'tsp'), may hold values from -6 to 6
- attn_out: bfloat16 [4, 1024, 4096], P('dp', None, 'ctx'), may hold values from -6 to 6
- out_weight: bfloat16 [4096, 8192], P('ctx', 'tsp'), may hold values from -0.0625 to 0.0625
- query: bfloat16 [4, 1024, 4096], P('dp', 'tsp', 'ctx'), may hold values from -128 to 128
- keys: bfloat16 [4, 1024, 512], P('dp'), may hold values from -128 to 128
- values: bfloat16 [4, 1024, 512], P('dp'), may hold values from -6 to 6
- segment_ids: int32 [4, 1024], P('dp'), may hold values from 0 to 7, never falling along the last dimension, each value on 1 to 256 neighbouring positions
- tile_live: int32 [4, 8, 8], P('dp'), may hold values 0 or 1
Outputs:
- grad_query: bfloat16 [4, 1024, 4096], P('dp', 'tsp', 'ctx')
- grad_keys: bfloat16 [4, 1024, 512], P('dp', ('ctx', 'tsp'))
- grad_values: bfloat16 [4, 1024, 512], P('dp', ('ctx', 'tsp'))
- grad_weight: float32 [4096, 8192], P('ctx', 'tsp')
Inputs may be any that keep to these rules, and one draw needn't show every extreme that they name: `segment_ids`: segment numbers never fall along a row and segment 0 is the source document; each segment has 1 to 256 tokens, one exactly that many.
All inputs are finite; a program needn't handle non-finite values. No bound on the sum of `tile_live` on one device may be relied on, other than what follows from the above.
Results may differ from a plain program's by a relative error of at most 0.0058.
Values may be sent and summed in bfloat16 or wider, within the bound.
A program may use at most 128 MiB of HBM per device.

v0:
```python
import math
import jax
import jax.numpy as jnp
from jax import lax
from jax.sharding import PartitionSpec as P

HEADS = 32
KV_HEADS = 4
HEAD_DIM = 128
TILE = 128


def merge_group(tensor_in):
    row_count = tensor_in.shape[0]
    folded = tensor_in.reshape(row_count, KV_HEADS, HEADS // KV_HEADS, HEAD_DIM).sum(axis=2)
    return folded.reshape(row_count, KV_HEADS * HEAD_DIM)


def per_device(grad_out, attn_out, out_weight, query, keys, values, segment_ids, tile_live):
    score_scale = 1.0 / math.sqrt(HEAD_DIM)
    out_all = attn_out[0]
    seq_len = out_all.shape[0]
    feat_width = out_all.shape[1]
    dy_block = lax.all_gather(grad_out, "ctx", axis=1, tiled=True)[0]
    proj_rows = lax.dot_general(
        dy_block, out_weight, (((1,), (1,)), ((), ())), preferred_element_type=jnp.float32
    )
    grad_part = proj_rows
    weight_part = lax.dot_general(
        out_all, dy_block, (((0,), (0,)), ((), ())), preferred_element_type=jnp.float32
    )
    grad_part, weight_part = (grad_part, weight_part)
    grad_weight = lax.psum(weight_part, "dp")
    out_grad = lax.psum_scatter(grad_part, "tsp", scatter_dimension=0, tiled=True).astype(
        jnp.bfloat16
    )
    quarter = out_grad.shape[0]
    row_start = lax.axis_index("tsp") * quarter
    heads_dev = feat_width // HEAD_DIM
    group_size = HEADS // KV_HEADS
    head_ids = lax.axis_index("ctx") * heads_dev + jnp.arange(heads_dev, dtype=jnp.int32)
    kv_ids = head_ids // group_size
    query_pos = row_start + jnp.arange(quarter, dtype=jnp.int32)
    key_pos = jnp.arange(seq_len, dtype=jnp.int32)
    tile_count = seq_len // TILE
    tile_rows = lax.dynamic_slice_in_dim(tile_live[0], row_start // TILE, quarter // TILE, 0)
    tile_mask = (
        jnp.broadcast_to(
            tile_rows[:, None, :, None], (quarter // TILE, TILE, tile_count, TILE)
        ).reshape(quarter, seq_len)
        == 1
    )
    same_tile = query_pos[:, None] // TILE == key_pos[None, :] // TILE
    segments = segment_ids[0]
    query_seg = lax.dynamic_slice_in_dim(segments, row_start, quarter, 0)
    same_doc = (segments[None, :] == query_seg[:, None]) | (segments[None, :] == 0)
    allowed = (tile_mask | same_tile) & same_doc & (key_pos[None, :] <= query_pos[:, None])

    def split_heads(tensor_in):
        return tensor_in.reshape(tensor_in.shape[0], heads_dev, HEAD_DIM).transpose(1, 0, 2)

    query_heads = split_heads(query[0])
    grad_heads = split_heads(out_grad)
    output_heads = split_heads(lax.dynamic_slice_in_dim(out_all, row_start, quarter, 0))
    key_table = keys[0].reshape(seq_len, KV_HEADS, HEAD_DIM)
    value_table = values[0].reshape(seq_len, KV_HEADS, HEAD_DIM)

    def one_head(head_items):
        query_head, grad_head, output_head, kv_index = head_items
        key_head = lax.dynamic_index_in_dim(key_table, kv_index, 1, keepdims=False)
        value_head = lax.dynamic_index_in_dim(value_table, kv_index, 1, keepdims=False)
        scores = (
            lax.dot_general(
                query_head, key_head, (((1,), (1,)), ((), ())), preferred_element_type=jnp.float32
            )
            * score_scale
        )
        scores = jnp.where(allowed, scores, -jnp.inf)
        row_max = jnp.max(scores, axis=1, keepdims=True)
        lse = row_max + jnp.log(jnp.sum(jnp.exp(scores - row_max), axis=1, keepdims=True))
        probs_f = jnp.where(allowed, jnp.exp(scores - lse), 0.0)
        probs = probs_f.astype(jnp.bfloat16)
        value_term = lax.dot_general(
            probs, grad_head, (((0,), (0,)), ((), ())), preferred_element_type=jnp.float32
        )
        dprobs = lax.dot_general(
            grad_head, value_head, (((1,), (1,)), ((), ())), preferred_element_type=jnp.float32
        )
        delta = jnp.sum(
            grad_head.astype(jnp.float32) * output_head.astype(jnp.float32), axis=1, keepdims=True
        )
        dscores = (probs_f * (dprobs - delta)).astype(jnp.bfloat16)
        query_grad = (
            jnp.dot(dscores, key_head, preferred_element_type=jnp.float32) * score_scale
        ).astype(jnp.bfloat16)
        key_term = (
            lax.dot_general(
                dscores, query_head, (((0,), (0,)), ((), ())), preferred_element_type=jnp.float32
            )
            * score_scale
        )
        return (query_grad, key_term, value_term)

    query_grads, key_terms, value_terms = lax.map(
        one_head, (query_heads, grad_heads, output_heads, kv_ids)
    )
    grad_query = query_grads.transpose(1, 0, 2).reshape(quarter, feat_width)
    key_cols = key_terms.transpose(1, 0, 2).reshape(seq_len, feat_width)
    value_cols = value_terms.transpose(1, 0, 2).reshape(seq_len, feat_width)
    key_recv, value_recv = (
        lax.all_to_all(key_cols, "ctx", split_axis=0, concat_axis=1, tiled=True),
        lax.all_to_all(value_cols, "ctx", split_axis=0, concat_axis=1, tiled=True),
    )
    key_part, value_part = (
        lax.psum_scatter(merge_group(key_recv), "tsp", scatter_dimension=0, tiled=True),
        lax.psum_scatter(merge_group(value_recv), "tsp", scatter_dimension=0, tiled=True),
    )
    grad_keys = key_part.astype(jnp.bfloat16)[None]
    grad_values = value_part.astype(jnp.bfloat16)[None]
    return (grad_query[None], grad_keys, grad_values, grad_weight)


def solution(mesh):
    placed = (
        P("dp", "ctx", "tsp"),
        P("dp", None, "ctx"),
        P("ctx", "tsp"),
        P("dp", "tsp", "ctx"),
        P("dp", None, None),
        P("dp", None, None),
        P("dp", None),
        P("dp", None, None),
    )
    return jax.shard_map(
        per_device,
        mesh=mesh,
        in_specs=placed,
        out_specs=(
            P("dp", "tsp", "ctx"),
            P("dp", ("ctx", "tsp"), None),
            P("dp", ("ctx", "tsp"), None),
            P("ctx", "tsp"),
        ),
        check_vma=False,
    )
```

profile of v0, /device:TPU:0, one launch (start us, length us, event | category | flops | bytes accessed | tf_op | source)
XLA Modules:
  0.0 900.4 jit_solution(15618256980744114519)
XLA Ops:
  8.0 154.0 %all-gather.2.cloned.1.call-done = bf16[1,1024,4096]{2,1,0:T(8,128)(2,1)} async-done(((bf16[1,256,4096]{2,1,0:T(8,128)(2,1)}), bf16[1,1024,4096]{2,1,0:T(8,128)(2,1)}) %all-gather.2.cloned.1.call-update) | async-done | bytes 8388624 | tf_op jit(solution)/shard_map/all_gather | solution.py:24
  161.9 15.1 %fusion.38 = f32[1024,1024]{1,0:T(8,128)} fusion(bf16[1024,4096]{1,0:T(8,128)(2,1)} %param.12, bf16[1,1024,4096]{2,1,0:T(8,128)(2,1)} %all-gather.2.cloned.1.call-done), kind=kOutput, calls=%fused_computation.47 | convolution fusion | flops 8589934592 | bytes 20971520 | tf_op jit(solution)/shard_map/dot_general | solution.py:25
  177.2 1.3 copy.66
  178.5 2.4 copy.46
  182.3 2.3 copy.49
  184.7 45.1 %reduce-scatter.4.cloned.1.call-done = f32[512,1024]{1,0:T(8,128)} async-done(((f32[1024,1024]{1,0:T(8,128)}), f32[512,1024]{1,0:T(8,128)}) %reduce-scatter.4.cloned.1.call-update) | async-done | bytes 2097168 | tf_op jit(solution)/shard_map/reduce_scatter | solution.py:34
  229.7 1.7 bitcast_bitcast_fusion
  231.5 129.6 %while.15 = (s32[]{:T(128)}, bf16[8,512,128]{2,1,0:T(8,128)(2,1)}, f32[8,1024,128]{2,1,0:T(8,128)}, f32[8,1024,128]{2,1,0:T(8,128)}, bf16[8,512,128]{1,2,0:T(8,1...) while((s32[]{:T(128)}, bf16[8,512,128]{2,1,0:T(8,128)(2,1)}, ...), condition=%wide.region_5.6_spmd.clone, body=%wide.region_1.5_spmd.clone.sunk | while | flops 689437696 | bytes 16977196 | solution.py:104
  235.4 2.4 fusion.73
  238.3 2.7 multiply_convert_fusion.2
  241.1 2.1 fusion.75
  243.1 2.4 fusion.77
  245.5 2.2 fusion.76
  251.6 2.4 fusion.73
  254.5 2.7 multiply_convert_fusion.2
  257.3 2.1 fusion.75
  259.3 2.4 fusion.77
  261.8 2.2 fusion.76
  267.9 2.4 fusion.73
  270.8 2.7 multiply_convert_fusion.2
  273.5 2.1 fusion.75
  275.6 2.4 fusion.77
  278.0 2.2 fusion.76
  284.1 2.4 fusion.73
  287.0 2.7 multiply_convert_fusion.2
  289.7 2.1 fusion.75
  291.8 2.4 fusion.77
  294.1 2.2 fusion.76
  300.3 2.4 fusion.73
  303.2 2.7 multiply_convert_fusion.2
  305.9 2.1 fusion.75
  308.0 2.4 fusion.77
  310.4 2.2 fusion.76
  316.5 2.4 fusion.73
  319.4 2.7 multiply_convert_fusion.2
  322.1 2.1 fusion.75
  324.2 2.4 fusion.77
  326.5 2.2 fusion.76
  332.7 2.4 fusion.73
  335.6 2.7 multiply_convert_fusion.2
  338.3 2.1 fusion.75
  340.4 2.4 fusion.77
  342.7 2.2 fusion.76
  348.9 2.4 fusion.73
  351.7 2.7 multiply_convert_fusion.2
  354.5 2.1 fusion.75
  356.5 2.4 fusion.77
  358.9 2.2 fusion.76
  361.1 6.6 copy.58
  367.7 4.9 all_to_all.27
  372.6 4.9 all-to-all-start.1
  377.5 6.5 copy.56
  384.0 4.9 all_to_all.24
  388.9 81.9 %all-to-all-done.1 = f32[4,256,1024]{2,1,0:T(8,128)} async-done(((f32[4,256,1024]{2,1,0:T(8,128)}), f32[4,256,1024]{2,1,0:T(8,128)}, u32[]{:S(2)}, u32[]{:S(2)}) %all-to-all-start.1) | async-done | bytes 4194336 | tf_op jit(solution)/shard_map/all_to_all | solution.py:112
  470.8 4.9 all-to-all-start
  475.8 5.1 copy.70
  480.9 3.2 reduce_sum.37
  485.2 83.3 %all-to-all-done = f32[4,256,1024]{2,1,0:T(8,128)} async-done(((f32[4,256,1024]{2,1,0:T(8,128)}), f32[4,256,1024]{2,1,0:T(8,128)}, u32[]{:S(2)}, u32[]{:S(2)}) %all-to-all-start) | async-done | bytes 4194336 | tf_op jit(solution)/shard_map/all_to_all | solution.py:111
  568.5 5.2 copy.69
  573.7 3.2 reduce_sum.36
  578.0 15.0 %fusion.36 = f32[1024,4096]{1,0:T(8,128)} fusion(bf16[1,1024,4096]{2,1,0:T(8,128)(2,1)} %all-gather.2.cloned.1.call-done, bf16[1,1024,1024]{2,1,0:T(8,128)(2,1)S(1)} %copy-done), kind=kOutput, calls=%fused_computation.45 | convolution fusion | flops 8589934592 | bytes 27262976 | tf_op jit(solution)/shard_map/dot_general | solution.py:29
  593.0 1.9 copy.55
  599.7 282.5 %all-reduce.2.cloned.1.call-done = f32[1024,4096]{1,0:T(8,128)} async-done(((f32[1024,4096]{1,0:T(8,128)}), f32[1024,4096]{1,0:T(8,128)}) %all-reduce.2.cloned.1.call-update) | async-done | bytes 16777232 | tf_op jit(solution)/shard_map/psum | solution.py:33
  882.2 11.7 %copy.104 = f32[1024,4096]{1,0:T(8,128)} copy(f32[1024,4096]{1,0:T(8,128)} %all-reduce.2.cloned.1.call-done) | data formatting | bytes 33554432
  (94 shorter events, 29.3 us)
Async XLA Ops:
  7.2 169.9 %copy-start = (bf16[1,1024,1024]{2,1,0:T(8,128)(2,1)S(1)}, bf16[1,1024,1024]{2,1,0:T(8,128)(2,1)}, u32[]{:S(2)}) copy-start(bf16[1,1024,1024]{2,1,0:T(8,128)(2,1)} %param.11) | copy-start | bytes 6291460
  7.2 154.7 %all-gather.2.cloned.1.call-start = ((), (), s32[]{:S(2)}) async-start(), calls=%async_computation.5 | async-start | bytes 10485760 | tf_op jit(solution)/shard_map/all_gather | solution.py:24
  7.9 221.8 %reduce-scatter.4.cloned.1.call-start = ((), (), s32[]{:S(2)}) async-start(), calls=%async_computation.6 | async-start | bytes 6291456 | tf_op jit(solution)/shard_map/reduce_scatter | solution.py:34
  178.5 2.4 copy-start.1
  180.9 3.6 copy-start.3
  180.9 3.7 copy-start.2
  372.6 98.3 %all-to-all-start.1 = ((f32[4,256,1024]{2,1,0:T(8,128)}), f32[4,256,1024]{2,1,0:T(8,128)}, u32[]{:S(2)}, u32[]{:S(2)}) async-start(f32[4,256,1024]{2,1,0:T(8,128)} %all_to_all.27), calls=%async_computation.3 | async-start | bytes 8388608 | tf_op jit(solution)/shard_map/all_to_all | solution.py:112
  470.8 97.7 %all-to-all-start = ((f32[4,256,1024]{2,1,0:T(8,128)}), f32[4,256,1024]{2,1,0:T(8,128)}, u32[]{:S(2)}, u32[]{:S(2)}) async-start(f32[4,256,1024]{2,1,0:T(8,128)} %all_to_all.24), calls=%async_computation.1 | async-start | bytes 8388608 | tf_op jit(solution)/shard_map/all_to_all | solution.py:111
  475.8 120.4 %reduce-scatter.8.cloned.1.call-start = ((), (), s32[]{:S(2)}) async-start(), calls=%async_computation.8 | async-start | bytes 786432 | tf_op jit(solution)/shard_map/reduce_scatter | solution.py:116
  485.1 112.8 %reduce-scatter.6.cloned.1.call-start = ((), (), s32[]{:S(2)}) async-start(), calls=%async_computation.7 | async-start | bytes 786432 | tf_op jit(solution)/shard_map/reduce_scatter | solution.py:115
  578.0 304.2 %all-reduce.2.cloned.1.call-start = ((), (), s32[]{:S(2)}) async-start(), calls=%async_computation.9 | async-start | bytes 33554432 | tf_op jit(solution)/shard_map/psum | solution.py:33
Sparse Core Ops, SparseCore 0:
  9.6 152.3 all-gather.1
  177.1 52.5 reduce-scatter.3
  485.3 15.0 reduce-scatter.7
  578.1 12.7 reduce-scatter.5
  593.8 288.3 all-reduce.1
where the time goes:
time: 902 us; the launch traced here: 900 us
  waiting for transfers between devices  648 us (72%)
  matrix products  124 us (14%)
  local copies, waits for them, and re-layouts  73.7 us (8%)
  loops' own time  15.8 us (2%)
  other arithmetic  15.5 us (2%)
  between operations  13.9 us (2%)
  starting transfers between devices  10.1 us (1%)
    psum x1, waiting for transfers between devices, per_device(): grad_weight = lax.psum(weight_part, 'dp')  282 us
    all_gather x1, waiting for transfers between devices, per_device(): dy_block = lax.all_gather(grad_out, 'ctx', axis=1, tiled=True)[0]  154 us
    all_to_all x1, waiting for transfers between devices, per_device(): lax.all_to_all(key_cols, 'ctx', split_axis=0, concat_axis=1, tiled=True)  83.3 us
    all_to_all x1, waiting for transfers between devices, per_device(): lax.all_to_all(value_cols, 'ctx', split_axis=0, concat_axis=1, tiled=True)  81.9 us
    reduce_scatter x1, waiting for transfers between devices, per_device(): lax.psum_scatter(grad_part, 'tsp', scatter_dimension=0, tiled=True)  45.1 us
    unnamed x17, local copies, waits for them, and re-layouts  31 us
    dot_general x8, matrix products, one_head(): lax.dot_general(grad_head, value_head, (((1,), (1,)), ((), ())), preferre...  21.9 us
    dot_general x8, matrix products, one_head(): lax.dot_general(probs, grad_head, (((0,), (0,)), ((), ())), preferred_ele...  19.1 us
  transfers between devices with their start and end apart: 7, of which 5 were waited for; matrix products, arithmetic and copies ran while one was open for 6% of the time, Pallas kernels for 0%

commit v1 on v0

--- a/solution.py
+++ b/solution.py
@@ -30,7 +30,11 @@
         out_all, dy_block, (((0,), (0,)), ((), ())), preferred_element_type=jnp.float32
     )
     grad_part, weight_part = (grad_part, weight_part)
-    grad_weight = lax.psum(weight_part, "dp")
+    grad_weight = weight_part
+    for hop in (1, 2):
+        grad_weight = grad_weight + lax.ppermute(
+            grad_weight, "dp", [(dev, dev ^ hop) for dev in range(4)]
+        )
     out_grad = lax.psum_scatter(grad_part, "tsp", scatter_dimension=0, tiled=True).astype(
         jnp.bfloat16
     )

time: 902 us -> 651 us (0.72)
  waiting for transfers between devices: 648 us -> 377 us
  other arithmetic: 15.5 us -> 51.4 us
  local copies, waits for them, and re-layouts: 73.7 us -> 58.7 us
    psum x1 -> x0, waiting for transfers between devices: 282 us -> none  [per_device(): grad_weight = lax.psum(weight_part, 'dp')]
    add x0 -> x2, other arithmetic: none -> 36 us  [per_device(): grad_weight + lax.ppermute(grad_weight, 'dp', [(dev, dev ^ hop) for dev i...]
    unnamed x17 -> x26, local copies, waits for them, and re-layouts: 31 us -> 17.1 us
  transfers between devices with their start and end apart: 7 -> 8, of which waited for: 5 -> 6; matrix products, arithmetic and copies ran while one was open for 6% -> 26% of each run, Pallas kernels for 0% -> 0%
where the time goes in v1:
time: 651 us; the launch traced here: 649 us
  waiting for transfers between devices  377 us (58%)
  matrix products  121 us (19%)
  local copies, waits for them, and re-layouts  58.7 us (9%)
  other arithmetic  51.4 us (8%)
  loops' own time  15.8 us (2%)
  between operations  14 us (2%)
  starting transfers between devices  11.6 us (2%)
    all_gather x1, waiting for transfers between devices, per_device(): dy_block = lax.all_gather(grad_out, 'ctx', axis=1, tiled=True)[0]  154 us
    all_to_all x1, waiting for transfers between devices, per_device(): lax.all_to_all(key_cols, 'ctx', split_axis=0, concat_axis=1, tiled=True)  83 us
    all_to_all x1, waiting for transfers between devices, per_device(): lax.all_to_all(value_cols, 'ctx', split_axis=0, concat_axis=1, tiled=True)  81.6 us
    reduce_scatter x1, waiting for transfers between devices, per_device(): lax.psum_scatter(grad_part, 'tsp', scatter_dimension=0, tiled=True)  47.3 us
    add x2, other arithmetic, per_device(): grad_weight + lax.ppermute(grad_weight, 'dp', [(dev, dev ^ hop) for dev i...  36 us
    dot_general x8, matrix products, one_head(): lax.dot_general(grad_head, value_head, (((1,), (1,)), ((), ())), preferre...  21.7 us
    dot_general x8, matrix products, one_head(): lax.dot_general(query_head, key_head, (((1,), (1,)), ((), ())), preferred...  18.9 us
    dot_general x8, matrix products, one_head(): lax.dot_general(probs, grad_head, (((0,), (0,)), ((), ())), preferred_ele...  18.8 us
  transfers between devices with their start and end apart: 8, of which 6 were waited for; matrix products, arithmetic and copies ran while one was open for 26% of the time, Pallas kernels for 0%

profile of v1, /device:TPU:0, one launch (start us, length us, event | category | flops | bytes accessed | tf_op | source)
XLA Modules:
  0.0 648.7 jit_solution(1295512713253820032)
XLA Ops:
  8.0 154.0 %all-gather.2.cloned.1.call-done = bf16[1,1024,4096]{2,1,0:T(8,128)(2,1)} async-done(((bf16[1,256,4096]{2,1,0:T(8,128)(2,1)}), bf16[1,1024,4096]{2,1,0:T(8,128)(2,1)}) %all-gather.2.cloned.1.call-update) | async-done | bytes 8388624 | tf_op jit(solution)/shard_map/all_gather | solution.py:24
  161.9 14.9 %fusion.36 = f32[1024,4096]{1,0:T(8,128)} fusion(bf16[1,1024,4096]{2,1,0:T(8,128)(2,1)} %all-gather.2.cloned.1.call-done, bf16[1,1024,1024]{2,1,0:T(8,128)(2,1)S(1)} %copy-done), kind=kOutput, calls=%fused_computation.45 | convolution fusion | flops 8589934592 | bytes 27262976 | tf_op jit(solution)/shard_map/dot_general | solution.py:29
  176.8 12.6 %fusion.38 = f32[1024,1024]{1,0:T(8,128)} fusion(bf16[1024,4096]{1,0:T(8,128)(2,1)} %param.12, bf16[1,1024,4096]{2,1,0:T(8,128)(2,1)S(1)} %copy-done.8), kind=kOutput, calls=%fused_computation.47 | convolution fusion | flops 8589934592 | bytes 20971520 | tf_op jit(solution)/shard_map/dot_general | solution.py:25
  190.9 1.3 copy.46
  195.0 47.3 %reduce-scatter.4.cloned.1.call-done = f32[512,1024]{1,0:T(8,128)} async-done(((f32[1024,1024]{1,0:T(8,128)}), f32[512,1024]{1,0:T(8,128)}) %reduce-scatter.4.cloned.1.call-update) | async-done | bytes 2097168 | tf_op jit(solution)/shard_map/reduce_scatter | solution.py:38
  242.3 1.7 bitcast_bitcast_fusion
  244.0 17.9 %add.74 = f32[1024,4096]{1,0:T(8,128)} add(f32[1024,4096]{1,0:T(8,128)} %fusion.36, f32[1024,4096]{1,0:T(8,128)} %collective-permute-done) | non-fusion elementwise | flops 4194304 | bytes 50331648 | tf_op jit(solution)/shard_map/add | solution.py:35
  262.0 1.5 collective-permute-start.1
  263.5 128.8 %while.15 = (s32[]{:T(128)}, bf16[8,512,128]{2,1,0:T(8,128)(2,1)}, f32[8,1024,128]{2,1,0:T(8,128)}, f32[8,1024,128]{2,1,0:T(8,128)}, bf16[8,512,128]{1,2,0:T(8,1...) while((s32[]{:T(128)}, bf16[8,512,128]{2,1,0:T(8,128)(2,1)}, ...), condition=%wide.region_5.6_spmd.clone, body=%wide.region_1.5_spmd.clone.sunk | while | flops 689437696 | bytes 16977196 | solution.py:108
  267.4 2.4 fusion.73
  270.3 2.7 multiply_convert_fusion.2
  273.0 2.1 fusion.75
  275.0 2.3 fusion.77
  277.4 2.2 fusion.76
  283.5 2.4 fusion.73
  286.4 2.7 multiply_convert_fusion.2
  289.1 2.1 fusion.75
  291.1 2.4 fusion.77
  293.5 2.2 fusion.76
  299.6 2.4 fusion.73
  302.5 2.7 multiply_convert_fusion.2
  305.2 2.1 fusion.75
  307.2 2.4 fusion.77
  309.6 2.2 fusion.76
  315.7 2.4 fusion.73
  318.6 2.7 multiply_convert_fusion.2
  321.3 2.1 fusion.75
  323.4 2.3 fusion.77
  325.7 2.2 fusion.76
  331.8 2.4 fusion.73
  334.7 2.7 multiply_convert_fusion.2
  337.4 2.1 fusion.75
  339.4 2.3 fusion.77
  341.8 2.2 fusion.76
  347.9 2.4 fusion.73
  350.7 2.7 multiply_convert_fusion.2
  353.5 2.1 fusion.75
  355.5 2.4 fusion.77
  357.9 2.2 fusion.76
  364.0 2.4 fusion.73
  366.9 2.7 multiply_convert_fusion.2
  369.6 2.1 fusion.75
  371.7 2.3 fusion.77
  374.0 2.2 fusion.76
  380.1 2.4 fusion.73
  382.9 2.7 multiply_convert_fusion.2
  385.7 2.1 fusion.75
  387.7 2.4 fusion.77
  390.1 2.2 fusion.76
  392.3 6.6 %copy.58 = f32[1024,8,128]{2,1,0:T(8,128)} copy(f32[1024,8,128]{2,0,1:T(8,128)} %bitcast.153) | data formatting | bytes 8388608 | tf_op jit(solution)/shard_map/transpose | solution.py:113
  398.8 4.9 all_to_all.27
  403.8 4.9 all-to-all-start.1
  408.7 6.6 %copy.56 = f32[1024,8,128]{2,1,0:T(8,128)} copy(f32[1024,8,128]{2,0,1:T(8,128)} %bitcast.154) | data formatting | bytes 8388608 | tf_op jit(solution)/shard_map/transpose | solution.py:112
  415.2 4.9 all_to_all.24
  420.1 81.6 %all-to-all-done.1 = f32[4,256,1024]{2,1,0:T(8,128)} async-done(((f32[4,256,1024]{2,1,0:T(8,128)}), f32[4,256,1024]{2,1,0:T(8,128)}, u32[]{:S(2)}, u32[]{:S(2)}) %all-to-all-start.1) | async-done | bytes 4194336 | tf_op jit(solution)/shard_map/all_to_all | solution.py:116
  501.7 4.8 all-to-all-start
  506.8 5.1 copy.70
  512.0 3.2 reduce_sum.37
  516.3 83.0 %all-to-all-done = f32[4,256,1024]{2,1,0:T(8,128)} async-done(((f32[4,256,1024]{2,1,0:T(8,128)}), f32[4,256,1024]{2,1,0:T(8,128)}, u32[]{:S(2)}, u32[]{:S(2)}) %all-to-all-start) | async-done | bytes 4194336 | tf_op jit(solution)/shard_map/all_to_all | solution.py:115
  599.3 5.1 copy.69
  604.5 3.3 reduce_sum.36
  612.5 8.3 %reduce-scatter.6.cloned.1.call-done = f32[128,512]{0,1:T(8,128)} async-done(((f32[256,512]{0,1:T(8,128)}), f32[128,512]{0,1:T(8,128)}) %reduce-scatter.6.cloned.1.call-update) | async-done | bytes 262160 | tf_op jit(solution)/shard_map/reduce_scatter | solution.py:119
  622.5 1.6 collective-permute-done.1
  624.1 18.1 %add.75 = f32[1024,4096]{1,0:T(8,128)} add(f32[1024,4096]{1,0:T(8,128)} %add.74, f32[1024,4096]{1,0:T(8,128)} %collective-permute-done.1) | non-fusion elementwise | flops 4194304 | bytes 50331648 | tf_op jit(solution)/shard_map/add | solution.py:35
  (106 shorter events, 32.5 us)
Async XLA Ops:
  7.2 154.8 %copy-start = (bf16[1,1024,1024]{2,1,0:T(8,128)(2,1)S(1)}, bf16[1,1024,1024]{2,1,0:T(8,128)(2,1)}, u32[]{:S(2)}) copy-start(bf16[1,1024,1024]{2,1,0:T(8,128)(2,1)} %param.11) | copy-start | bytes 6291460
  7.2 154.7 %all-gather.2.cloned.1.call-start = ((), (), s32[]{:S(2)}) async-start(), calls=%async_computation.5 | async-start | bytes 10485760 | tf_op jit(solution)/shard_map/all_gather | solution.py:24
  7.9 234.4 %reduce-scatter.4.cloned.1.call-start = ((), (), s32[]{:S(2)}) async-start(), calls=%async_computation.6 | async-start | bytes 6291456 | tf_op jit(solution)/shard_map/reduce_scatter | solution.py:38
  161.9 14.9 %copy-start.8 = (bf16[1,1024,4096]{2,1,0:T(8,128)(2,1)S(1)}, bf16[1,1024,4096]{2,1,0:T(8,128)(2,1)}, u32[]{:S(2)}) copy-start(bf16[1,1024,4096]{2,1,0:T(8,128)(2,1)} %all-gather.2.cloned.1.call-done) | copy-start | bytes 25165828
  176.8 67.2 %collective-permute-start = (f32[1024,4096]{1,0:T(8,128)}, f32[1024,4096]{1,0:T(8,128)}, u32[]{:S(2)}, u32[]{:S(2)}) collective-permute-start(f32[1024,4096]{1,0:T(8,128)} %fusion.36), channel_id=1, source_target_pairs={{0,8},{8,0},{16,24},{24,16},{1,9},{9,1},{17,25},{25,17},{2,10},{10... | collective-permute-start | bytes 50331656 | tf_op jit(solution)/shard_map/ppermute | solution.py:35
  189.6 1.4 copy-start.2
  189.6 2.7 copy-start.3
  190.9 2.7 copy-start.4
  192.3 2.6 copy-start.7
  192.3 2.7 copy-start.6
  262.0 362.1 %collective-permute-start.1 = (f32[1024,4096]{1,0:T(8,128)}, f32[1024,4096]{1,0:T(8,128)}, u32[]{:S(2)}, u32[]{:S(2)}) collective-permute-start(f32[1024,4096]{1,0:T(8,128)} %add.74), channel_id=1, source_target_pairs={{0,16},{8,24},{16,0},{24,8},{1,17},{9,25},{17,1},{25,9},{2,18},{10... | collective-permute-start | bytes 50331656 | tf_op jit(solution)/shard_map/ppermute | solution.py:35
  403.8 98.0 %all-to-all-start.1 = ((f32[4,256,1024]{2,1,0:T(8,128)}), f32[4,256,1024]{2,1,0:T(8,128)}, u32[]{:S(2)}, u32[]{:S(2)}) async-start(f32[4,256,1024]{2,1,0:T(8,128)} %all_to_all.27), calls=%async_computation.3 | async-start | bytes 8388608 | tf_op jit(solution)/shard_map/all_to_all | solution.py:116
  501.7 97.6 %all-to-all-start = ((f32[4,256,1024]{2,1,0:T(8,128)}), f32[4,256,1024]{2,1,0:T(8,128)}, u32[]{:S(2)}, u32[]{:S(2)}) async-start(f32[4,256,1024]{2,1,0:T(8,128)} %all_to_all.24), calls=%async_computation.1 | async-start | bytes 8388608 | tf_op jit(solution)/shard_map/all_to_all | solution.py:115
  506.6 104.1 %reduce-scatter.8.cloned.1.call-start = ((), (), s32[]{:S(2)}) async-start(), calls=%async_computation.8 | async-start | bytes 786432 | tf_op jit(solution)/shard_map/reduce_scatter | solution.py:120
  516.2 104.5 %reduce-scatter.6.cloned.1.call-start = ((), (), s32[]{:S(2)}) async-start(), calls=%async_computation.7 | async-start | bytes 786432 | tf_op jit(solution)/shard_map/reduce_scatter | solution.py:119
  604.5 4.3 copy-start.5
  624.1 18.1 %copy-start.1 = (bf16[1,1024,1024]{2,1,0:T(8,128)(2,1)S(1)}, bf16[1,1024,1024]{2,1,0:T(8,128)(2,1)}, u32[]{:S(2)}) copy-start(bf16[1,1024,1024]{2,1,0:T(8,128)(2,1)} %param.11) | copy-start | bytes 6291460
Sparse Core Ops, SparseCore 0:
  9.6 152.3 all-gather.1
  189.6 52.6 reduce-scatter.3
  516.4 13.8 reduce-scatter.7
  608.9 11.8 reduce-scatter.5
